TPU v7x, 256 devices: a whole 4x4x8 slice. The times are simulated.
256 devices in a mesh: lat: 64 (over x, y_hi, z), lon: 4 (over y_lo, core).
Axes of the slice: x: 4, y: 4 (y_hi: 2, y_lo: 2; y = y_hi * 2 + y_lo), z: 8, core: 2. Of those that a mesh axis runs over, the one named last changes fastest.
Arguments:
- tracer: float32 [32, 1536, 1152], P(None, 'lat', 'lon'), may hold values from -6 to 6
- wind_u: float32 [32, 1536, 1152], P(None, 'lat', 'lon'), may hold values from -2.5 to 2.5
- wind_v: float32 [32, 1536, 1152], P(None, 'lat', 'lon'), may hold values from -2.5 to 2.5
- ocean_temp: float32 [4, 2048, 3584], P(None, 'lat', 'lon'), may hold values from -6 to 6
- land_mask: int32 [2048, 3584], P('lat', 'lon'), may hold values 0 or 1
- remap_rows: int32 [2048, 3584], P('lat', 'lon'), may hold values from 0 to 1535, as said below
- remap_cols: int32 [2048, 3584], P('lat', 'lon'), may hold values from 0 to 1151, as said below
- polar_rows: int32 [192], replicated, may hold values from 0 to 1535, as said below
Outputs:
- tracer_out: float32 [32, 1536, 1152], P(None, 'lat', 'lon')
- ocean_out: float32 [4, 2048, 3584], P(None, 'lat', 'lon')
Inputs may be any that keep to these rules, and one draw needn't show every extreme that they name: `remap_rows`: for an ocean cell in row block b of 32 rows, an atmosphere row from b * 24 - 1 to (b + 1) * 24, within the grid. `remap_cols`: for an ocean cell in column block c of 896 columns, an atmosphere column from c * 288 - 1 to (c + 1) * 288, modulo 1152. `polar_rows`: distinct rows, each among the 192 rows nearest either pole.
All inputs are finite; a program needn't handle non-finite values. No bound on the sum of `land_mask` on one device may be relied on, other than what follows from the above.
Results may differ from a plain program's by a relative error of at most 0.0001.
Values sent between devices are 32-bit elements; how exact they have to be, the bound alone decides.
No kernel may reach another device: no remote copies, remote signals or barrier semaphores. Data moves between devices by JAX's collectives and lax.ppermute only.
A program may use at most 128 MiB of HBM per device.

v0:
```python
import math
import jax
import jax.numpy as jnp
from jax import lax
from jax.sharding import PartitionSpec as P

STEPS = 2
OSTEPS = 2
advect_coef = 0.2
diffuse_coef = 0.1
flux_coef = 0.25
ocean_diffuse = 0.15
vertical_mix = 0.2
highest = lax.Precision.HIGHEST


def padded_2(shard, sides, width, wrap):
    for axis, dim in sides:
        count, length = (lax.axis_size(axis), shard.shape[dim])
        up = [(i, (i + 1) % count) for i in range(count if wrap else count - 1)]
        down = [(j, i) for i, j in up]
        last = lax.slice_in_dim(shard, length - width, length, axis=dim)
        first = lax.slice_in_dim(shard, 0, width, axis=dim)
        before = lax.ppermute(last, axis, up)
        after = lax.ppermute(first, axis, down)
        shard = jnp.concatenate([before, shard, after], axis=dim)
    return shard


def damp_table(row_index, polar_rows, wave_numbers, lat_total, band_rows, lon_total):
    latitude_cos = jnp.sin(math.pi * (row_index.astype(jnp.float32) + 0.5) / lat_total)
    ratio = latitude_cos / math.sin(math.pi * band_rows / lat_total)
    wave_sine = jnp.sin(math.pi * wave_numbers / lon_total)
    safe_sine = jnp.where(wave_numbers > 0.5, wave_sine, 1.0)
    damping = jnp.where(
        wave_numbers[None, :] > 0.5, jnp.minimum(1.0, ratio[:, None] / safe_sine[None, :]), 1.0
    )
    listed = jnp.any(row_index[:, None] == polar_rows[None, :], axis=1)
    return jnp.where(listed[:, None], damping, 1.0)


def make_basis(lon_total):
    half_circle = lon_total // 2
    points = jnp.arange(lon_total, dtype=jnp.int32)
    cos_waves = jnp.arange(half_circle + 1, dtype=jnp.int32)
    sin_waves = jnp.arange(1, half_circle, dtype=jnp.int32)
    cos_phase = points[:, None] * cos_waves[None, :] % lon_total
    sin_phase = points[:, None] * sin_waves[None, :] % lon_total
    basis = jnp.concatenate(
        [
            jnp.cos(2.0 * math.pi * cos_phase.astype(jnp.float32) / lon_total),
            jnp.sin(2.0 * math.pi * sin_phase.astype(jnp.float32) / lon_total),
        ],
        axis=1,
    )
    waves_all = jnp.concatenate([cos_waves, sin_waves])
    wave_numbers = waves_all.astype(jnp.float32)
    weight = jnp.where(
        (waves_all == 0) | (waves_all == half_circle), 1.0 / lon_total, 2.0 / lon_total
    )
    return (basis, wave_numbers, weight)


def rim(field):
    wider = padded_2(field, (("lat", 1),), 1, False)
    return padded_2(wider, (("lon", 2),), 1, True)


def atmos_step(tracer_now, wind_u, wind_v):
    padded = rim(tracer_now)
    east_side = padded[:, 1:-1, 2:]
    west_side = padded[:, 1:-1, :-2]
    north_side = padded[:, 2:, 1:-1]
    south_side = padded[:, :-2, 1:-1]
    advect = wind_u * (east_side - west_side) + wind_v * (north_side - south_side)
    spread_sum = east_side + west_side + north_side + south_side - 4.0 * tracer_now
    return tracer_now - advect_coef * advect + diffuse_coef * spread_sum


def back_project(scaled, target_basis):
    return lax.dot_general(
        scaled,
        target_basis,
        (((1,), (1,)), ((), ())),
        precision=highest,
        preferred_element_type=jnp.float32,
    )


def ocean_step(temp, sea, air_temp, air_speed):
    top_level = temp[0] + sea * flux_coef * air_speed * (air_temp - temp[0])
    temp = jnp.concatenate([top_level[None], temp[1:]], axis=0)
    padded = rim(jnp.concatenate([temp, sea[None]], axis=0))
    level_count = temp.shape[0]
    temp_rim = padded[:level_count]
    sea_rim = padded[level_count]
    lateral = sea * (
        sea_rim[1:-1, 2:] * (temp_rim[:, 1:-1, 2:] - temp)
        + sea_rim[1:-1, :-2] * (temp_rim[:, 1:-1, :-2] - temp)
        + sea_rim[2:, 1:-1] * (temp_rim[:, 2:, 1:-1] - temp)
        + sea_rim[:-2, 1:-1] * (temp_rim[:, :-2, 1:-1] - temp)
    )
    temp = temp + ocean_diffuse * lateral
    upper = jnp.concatenate([temp[:1], temp[:-1]], axis=0)
    lower = jnp.concatenate([temp[1:], temp[-1:]], axis=0)
    return temp + vertical_mix * sea * (upper + lower - 2.0 * temp)


def per_device(tracer, wind_u, wind_v, ocean_temp, land_mask, remap_rows, remap_cols, polar_rows):
    levels, row_count, lon_local = tracer.shape
    lat_devices = lax.axis_size("lat")
    lon_devices = lax.axis_size("lon")
    lat_total = row_count * lat_devices
    lon_total = lon_local * lon_devices
    band_devices = lat_devices // 8
    band_rows = band_devices * row_count
    lat_place = lax.axis_index("lat")
    lon_place = lax.axis_index("lon")
    basis, wave_numbers, weight = make_basis(lon_total)
    own_basis = lax.dynamic_slice_in_dim(basis, lon_place * lon_local, lon_local, 0)
    own_rows = lat_place * row_count + jnp.arange(row_count, dtype=jnp.int32)
    line_count = levels * row_count
    tracer_now = tracer
    for step_index in range(STEPS):
        tracer_now = atmos_step(tracer_now, wind_u, wind_v)
        row_weights = (
            damp_table(own_rows, polar_rows, wave_numbers, lat_total, band_rows, lon_total)
            * weight[None, :]
        )
        lines = tracer_now.reshape(line_count, lon_local)
        coeffs = jnp.dot(
            lax.all_gather(lines, "lon", axis=1, tiled=True),
            basis,
            precision=highest,
            preferred_element_type=jnp.float32,
        )
        scaled = (coeffs.reshape(levels, row_count, lon_total) * row_weights[None]).reshape(
            line_count, lon_total
        )
        tracer_now = back_project(scaled, own_basis).reshape(levels, row_count, lon_local)
    bottom = jnp.stack(
        [tracer_now[levels - 1], jnp.abs(wind_u[levels - 1]) + jnp.abs(wind_v[levels - 1]) + 0.5]
    )
    bottom_rim = rim(bottom)
    local_row = remap_rows - lat_place * row_count + 1
    local_col = (remap_cols - lon_place * lon_local + 1) % lon_total
    flat_index = local_row * (lon_local + 2) + local_col
    picked = jnp.take(bottom_rim.reshape(2, -1), flat_index, axis=1)
    air_temp = picked[0]
    air_speed = picked[1]
    sea = land_mask.astype(jnp.float32)
    temp = ocean_temp
    for step_index in range(OSTEPS):
        temp = ocean_step(temp, sea, air_temp, air_speed)
    return (tracer_now, temp)


def solution(mesh):
    in_specs = (
        P(None, "lat", "lon"),
        P(None, "lat", "lon"),
        P(None, "lat", "lon"),
        P(None, "lat", "lon"),
        P("lat", "lon"),
        P("lat", "lon"),
        P("lat", "lon"),
        P(),
    )
    out_specs = (P(None, "lat", "lon"), P(None, "lat", "lon"))
    return jax.shard_map(
        per_device, mesh=mesh, in_specs=in_specs, out_specs=out_specs, check_vma=False
    )
```

profile of v0, /device:TPU:3, one launch (start us, length us, event | category | flops | bytes accessed | tf_op | source)
XLA Modules:
  0.0 390.3 jit_solution(18377480665657922847)
XLA Ops:
  8.5 3.7 collective-permute-start
  12.2 8.5 %collective-permute-start.1 = (f32[32,1,288]{2,1,0:T(1,128)S(1)}, f32[32,1,288]{2,1,0:T(1,128)S(1)}, u32[]{:S(2)}, u32[]{:S(2)}) collective-permute-start(f32[32,1,288]{2,1,0:T(1,128)S(1)} %get-tuple-element.13), channel_id=1, source_target_pairs={{4,0},{8,4},{12,8},{16,12},{20,16},{24,20},{28,24},{32,28},{36,32}... | collective-permute-start | bytes 110600 | tf_op jit(solution)/shard_map/ppermute | solution.py:25
  25.2 11.8 %collective-permute-done.2 = f32[32,26,1]{2,1,0:T(8,128)S(1)} collective-permute-done((f32[32,26,1]{2,1,0:T(8,128)S(1)}, f32[32,26,1]{2,1,0:T(8,128)S(1)}, u32[]{:S(2)}, u32[]{:S(2)}) %collective-permute-start.2) | collective-permute-done | bytes 3360 | tf_op jit(solution)/shard_map/ppermute | solution.py:25
  37.1 2.8 multiply_add_fusion.1
  41.8 11.0 %fusion.2 = f32[1152,577]{1,0:T(8,128)S(1)} fusion(), kind=kLoop, calls=%fused_computation.10 | loop fusion | flops 5982336 | bytes 2658816 | tf_op jit(solution)/shard_map/cos | solution.py:51
  52.9 12.6 %fusion.5 = f32[1152,575]{1,0:T(8,128)} fusion(s32[575]{0:T(1024)S(1)} %iota_add_fusion), kind=kLoop, calls=%fused_computation.13 | loop fusion | flops 5961600 | bytes 2651900 | tf_op jit(solution)/shard_map/sin | solution.py:52
  65.6 21.0 %all-gather.3.cloned.1.call-done = f32[768,1152]{0,1:T(8,128)} async-done(((f32[768,288]{0,1:T(8,128)}), f32[768,1152]{0,1:T(8,128)}) %all-gather.3.cloned.1.call-update) | async-done | bytes 3538960 | tf_op jit(solution)/shard_map/all_gather | solution.py:132
  86.5 21.0 %bitcast_multiply_fusion.1 = f32[768,1152]{1,0:T(8,128)S(1)} fusion(f32[768,1152]{0,1:T(8,128)} %all-gather.3.cloned.1.call-done, f32[1152,575]{1,0:T(8,128)} %fusion.5, f32[1152,577]{1,0:T(8,128)S(1)} %fusion.2, f32[24,1152]{1,0:T(8,128)S(1)} %fusion.87), kind=kOutput, calls=%fused_computation.5 | convolution fusion | flops 12232802304 | bytes 12496896 | tf_op jit(solution)/shard_map/dot_general | solution.py:131
  107.5 6.2 %fusion.13 = f32[32,24,288]{2,1,0:T(8,128)S(1)} fusion(f32[32,24,1152]{2,1,0:T(8,128)S(1)} %bitcast.57, s32[]{:T(128)S(6)} %select_n.72, f32[1152,577]{1,0:T(8,128)S(1)} %fusion.2, f32[1152,575]{1,0:T(8,128)S(1)} %copy-done), kind=kOutput, calls=%fused_computation.23 | convolution fusion | flops 3057979392 | bytes 9732100 | tf_op jit(solution)/shard_map/dot_general | solution.py:81
  113.8 3.3 collective-permute-start.4
  117.2 6.6 %collective-permute-start.5 = (f32[32,1,288]{2,1,0:T(1,128)S(1)}, f32[32,1,288]{2,1,0:T(1,128)S(1)}, u32[]{:S(2)}, u32[]{:S(2)}) collective-permute-start(f32[32,1,288]{2,1,0:T(1,128)S(1)} %get-tuple-element.11), channel_id=1, source_target_pairs={{4,0},{8,4},{12,8},{16,12},{20,16},{24,20},{28,24},{32,28},{36,32}... | collective-permute-start | bytes 110600 | tf_op jit(solution)/shard_map/ppermute | solution.py:25
  127.5 12.6 %collective-permute-done.6 = f32[32,26,1]{2,1,0:T(8,128)S(1)} collective-permute-done((f32[32,26,1]{2,1,0:T(8,128)S(1)}, f32[32,26,1]{2,1,0:T(8,128)S(1)}, u32[]{:S(2)}, u32[]{:S(2)}) %collective-permute-start.6) | collective-permute-done | bytes 3360 | tf_op jit(solution)/shard_map/ppermute | solution.py:25
  148.1 41.0 %all-gather.5.cloned.1.call-done = f32[768,1152]{0,1:T(8,128)} async-done(((f32[768,288]{0,1:T(8,128)}), f32[768,1152]{0,1:T(8,128)}) %all-gather.5.cloned.1.call-update) | async-done | bytes 3538960 | tf_op jit(solution)/shard_map/all_gather | solution.py:132
  189.1 21.0 %bitcast_multiply_fusion = f32[768,1152]{1,0:T(8,128)S(1)} fusion(f32[768,1152]{0,1:T(8,128)} %all-gather.5.cloned.1.call-done, f32[1152,575]{1,0:T(8,128)} %fusion.5, f32[1152,577]{1,0:T(8,128)S(1)} %fusion.2, f32[24,1152]{1,0:T(8,128)S(1)} %fusion.87), kind=kOutput, calls=%fused_computation.4 | convolution fusion | flops 12232802304 | bytes 12496896 | tf_op jit(solution)/shard_map/dot_general | solution.py:131
  210.0 4.1 %fusion.90 = f32[768,288]{0,1:T(8,128)S(1)} fusion(f32[768,1152]{1,0:T(8,128)S(1)} %bitcast_multiply_fusion, s32[]{:T(128)S(6)} %select_n.72, f32[1152,577]{1,0:T(8,128)S(1)} %fusion.2, f32[1152,575]{1,0:T(8,128)S(1)} %copy-done.1), kind=kOutput, calls=%fused_computation.184 | convolution fusion | flops 3057979392 | bytes 9732100 | tf_op jit(solution)/shard_map/dot_general | solution.py:81
  215.3 3.3 collective-permute-start.8
  218.6 6.6 %collective-permute-start.9 = (f32[2,1,288]{1,2,0:T(8,128)S(1)}, f32[2,1,288]{1,2,0:T(8,128)S(1)}, u32[]{:S(2)}, u32[]{:S(2)}) collective-permute-start(f32[2,1,288]{1,2,0:T(8,128)S(1)} %get-tuple-element.31), channel_id=1, source_target_pairs={{4,0},{8,4},{12,8},{16,12},{20,16},{24,20},{28,24},{32,28},{36,32}... | collective-permute-start | bytes 6920 | tf_op jit(solution)/shard_map/ppermute | solution.py:25
  225.4 5.3 %collective-permute-done.8 = f32[2,1,288]{1,2,0:T(8,128)S(1)} collective-permute-done((f32[2,1,288]{1,2,0:T(8,128)S(1)}, f32[2,1,288]{1,2,0:T(8,128)S(1)}, u32[]{:S(2)}, u32[]{:S(2)}) %collective-permute-start.8) | collective-permute-done | bytes 2336 | tf_op jit(solution)/shard_map/ppermute | solution.py:24
  236.8 2.7 copy.39
  239.5 97.5 %gather_fusion = f32[28672,2]{1,0:T(8,128)} fusion(f32[2,7540]{0,1:T(8,128)} %copy.39, s32[28672]{0:T(1024)S(1)} %broadcast_clamp_fusion), kind=kCustom, calls=%fused_computation | custom fusion | bytes 573440 | tf_op jit(solution)/shard_map/jit(_take)/gather | solution.py:148
  336.9 9.0 %copy.40 = f32[32,896,2]{1,0,2:T(8,128)S(1)} copy(f32[32,896,2]{2,1,0:T(8,128)} %bitcast.56) | data formatting | bytes 458752 | tf_op jit(solution)/shard_map/jit(_take)/gather | solution.py:148
  348.0 9.2 %collective-permute-start.13 = (f32[5,1,896]{2,1,0:T(1,128)S(1)}, f32[5,1,896]{2,1,0:T(1,128)S(1)}, u32[]{:S(2)}, u32[]{:S(2)}) collective-permute-start(f32[5,1,896]{2,1,0:T(1,128)S(1)} %get-tuple-element.20), channel_id=1, source_target_pairs={{4,0},{8,4},{12,8},{16,12},{20,16},{24,20},{28,24},{32,28},{36,32}... | collective-permute-start | bytes 53768 | tf_op jit(solution)/shard_map/ppermute | solution.py:25
  360.3 2.7 collective-permute-done.15
  366.6 9.0 %collective-permute-start.17 = (f32[5,1,896]{2,1,0:T(1,128)S(1)}, f32[5,1,896]{2,1,0:T(1,128)S(1)}, u32[]{:S(2)}, u32[]{:S(2)}) collective-permute-start(f32[5,1,896]{2,1,0:T(1,128)S(1)} %get-tuple-element.18), channel_id=1, source_target_pairs={{4,0},{8,4},{12,8},{16,12},{20,16},{24,20},{28,24},{32,28},{36,32}... | collective-permute-start | bytes 53768 | tf_op jit(solution)/shard_map/ppermute | solution.py:25
  (116 shorter events, 43.2 us)
Async XLA Ops:
  7.2 79.3 %all-gather.3.cloned.1.call-start = ((), (), s32[]{:S(2)}) async-start(), calls=%async_computation | async-start | bytes 4423680 | tf_op jit(solution)/shard_map/all_gather | solution.py:132
  7.2 29.9 %copy-start.3 = (f32[32,24,288]{2,1,0:T(8,128)S(1)}, f32[32,24,288]{2,1,0:T(8,128)}, u32[]{:S(2)}) copy-start(f32[32,24,288]{2,1,0:T(8,128)} %param.9) | copy-start | bytes 2654212
  8.5 28.6 %copy-start.2 = (f32[32,24,288]{2,1,0:T(8,128)S(1)}, f32[32,24,288]{2,1,0:T(8,128)}, u32[]{:S(2)}) copy-start(f32[32,24,288]{2,1,0:T(8,128)} %param.8) | copy-start | bytes 2654212
  8.5 12.2 %collective-permute-start = (f32[32,1,288]{2,1,0:T(1,128)S(1)}, f32[32,1,288]{2,1,0:T(1,128)S(1)}, u32[]{:S(2)}, u32[]{:S(2)}) collective-permute-start(f32[32,1,288]{2,1,0:T(1,128)S(1)} %get-tuple-element.12), channel_id=1, source_target_pairs={{0,4},{4,8},{8,12},{12,16},{16,20},{20,24},{24,28},{28,32},{32,36}... | collective-permute-start | bytes 110600 | tf_op jit(solution)/shard_map/ppermute | solution.py:24
  12.2 9.6 %collective-permute-start.1 = (f32[32,1,288]{2,1,0:T(1,128)S(1)}, f32[32,1,288]{2,1,0:T(1,128)S(1)}, u32[]{:S(2)}, u32[]{:S(2)}) collective-permute-start(f32[32,1,288]{2,1,0:T(1,128)S(1)} %get-tuple-element.13), channel_id=1, source_target_pairs={{4,0},{8,4},{12,8},{16,12},{20,16},{24,20},{28,24},{32,28},{36,32}... | collective-permute-start | bytes 110600 | tf_op jit(solution)/shard_map/ppermute | solution.py:25
  23.3 13.8 %collective-permute-start.2 = (f32[32,26,1]{2,1,0:T(8,128)S(1)}, f32[32,26,1]{2,1,0:T(8,128)S(1)}, u32[]{:S(2)}, u32[]{:S(2)}) collective-permute-start(f32[32,26,1]{2,1,0:T(8,128)S(1)} %get-tuple-element.9), channel_id=1, source_target_pairs={{1,0},{2,1},{3,2},{0,3},{5,4},{6,5},{7,6},{4,7},{9,8},{10,9},{11,1... | collective-permute-start | bytes 9992 | tf_op jit(solution)/shard_map/ppermute | solution.py:25
  24.9 12.2 %collective-permute-start.3 = (f32[32,26,1]{2,1,0:T(8,128)S(1)}, f32[32,26,1]{2,1,0:T(8,128)S(1)}, u32[]{:S(2)}, u32[]{:S(2)}) collective-permute-start(f32[32,26,1]{2,1,0:T(8,128)S(1)} %get-tuple-element.8), channel_id=1, source_target_pairs={{0,1},{1,2},{2,3},{3,0},{4,5},{5,6},{6,7},{7,4},{8,9},{9,10},{10,1... | collective-permute-start | bytes 9992 | tf_op jit(solution)/shard_map/ppermute | solution.py:24
  41.1 147.9 %all-gather.5.cloned.1.call-start = ((), (), s32[]{:S(2)}) async-start(), calls=%async_computation.1 | async-start | bytes 4423680 | tf_op jit(solution)/shard_map/all_gather | solution.py:132
  113.8 10.2 %collective-permute-start.4 = (f32[32,1,288]{2,1,0:T(1,128)S(1)}, f32[32,1,288]{2,1,0:T(1,128)S(1)}, u32[]{:S(2)}, u32[]{:S(2)}) collective-permute-start(f32[32,1,288]{2,1,0:T(1,128)S(1)} %get-tuple-element.10), channel_id=1, source_target_pairs={{0,4},{4,8},{8,12},{12,16},{16,20},{20,24},{24,28},{28,32},{32,36}... | collective-permute-start | bytes 110600 | tf_op jit(solution)/shard_map/ppermute | solution.py:24
  117.2 7.8 %collective-permute-start.5 = (f32[32,1,288]{2,1,0:T(1,128)S(1)}, f32[32,1,288]{2,1,0:T(1,128)S(1)}, u32[]{:S(2)}, u32[]{:S(2)}) collective-permute-start(f32[32,1,288]{2,1,0:T(1,128)S(1)} %get-tuple-element.11), channel_id=1, source_target_pairs={{4,0},{8,4},{12,8},{16,12},{20,16},{24,20},{28,24},{32,28},{36,32}... | collective-permute-start | bytes 110600 | tf_op jit(solution)/shard_map/ppermute | solution.py:25
  125.2 14.8 %collective-permute-start.6 = (f32[32,26,1]{2,1,0:T(8,128)S(1)}, f32[32,26,1]{2,1,0:T(8,128)S(1)}, u32[]{:S(2)}, u32[]{:S(2)}) collective-permute-start(f32[32,26,1]{2,1,0:T(8,128)S(1)} %get-tuple-element.7), channel_id=1, source_target_pairs={{1,0},{2,1},{3,2},{0,3},{5,4},{6,5},{7,6},{4,7},{9,8},{10,9},{11,1... | collective-permute-start | bytes 9992 | tf_op jit(solution)/shard_map/ppermute | solution.py:25
  126.5 13.5 %collective-permute-start.7 = (f32[32,26,1]{2,1,0:T(8,128)S(1)}, f32[32,26,1]{2,1,0:T(8,128)S(1)}, u32[]{:S(2)}, u32[]{:S(2)}) collective-permute-start(f32[32,26,1]{2,1,0:T(8,128)S(1)} %get-tuple-element.6), channel_id=1, source_target_pairs={{0,1},{1,2},{2,3},{3,0},{4,5},{5,6},{6,7},{7,4},{8,9},{9,10},{10,1... | collective-permute-start | bytes 9992 | tf_op jit(solution)/shard_map/ppermute | solution.py:24
  215.3 15.4 %collective-permute-start.8 = (f32[2,1,288]{1,2,0:T(8,128)S(1)}, f32[2,1,288]{1,2,0:T(8,128)S(1)}, u32[]{:S(2)}, u32[]{:S(2)}) collective-permute-start(f32[2,1,288]{1,2,0:T(8,128)S(1)} %get-tuple-element.30), channel_id=1, source_target_pairs={{0,4},{4,8},{8,12},{12,16},{16,20},{20,24},{24,28},{28,32},{32,36}... | collective-permute-start | bytes 6920 | tf_op jit(solution)/shard_map/ppermute | solution.py:24
  218.6 13.0 %collective-permute-start.9 = (f32[2,1,288]{1,2,0:T(8,128)S(1)}, f32[2,1,288]{1,2,0:T(8,128)S(1)}, u32[]{:S(2)}, u32[]{:S(2)}) collective-permute-start(f32[2,1,288]{1,2,0:T(8,128)S(1)} %get-tuple-element.31), channel_id=1, source_target_pairs={{4,0},{8,4},{12,8},{16,12},{20,16},{24,20},{28,24},{32,28},{36,32}... | collective-permute-start | bytes 6920 | tf_op jit(solution)/shard_map/ppermute | solution.py:25
  231.9 2.2 collective-permute-start.10
  233.1 3.3 collective-permute-start.11
  346.1 11.2 %collective-permute-start.12 = (f32[5,1,896]{2,1,0:T(1,128)S(1)}, f32[5,1,896]{2,1,0:T(1,128)S(1)}, u32[]{:S(2)}, u32[]{:S(2)}) collective-permute-start(f32[5,1,896]{2,1,0:T(1,128)S(1)} %get-tuple-element.21), channel_id=1, source_target_pairs={{0,4},{4,8},{8,12},{12,16},{16,20},{20,24},{24,28},{28,32},{32,36}... | collective-permute-start | bytes 53768 | tf_op jit(solution)/shard_map/ppermute | solution.py:24
  348.0 10.1 %collective-permute-start.13 = (f32[5,1,896]{2,1,0:T(1,128)S(1)}, f32[5,1,896]{2,1,0:T(1,128)S(1)}, u32[]{:S(2)}, u32[]{:S(2)}) collective-permute-start(f32[5,1,896]{2,1,0:T(1,128)S(1)} %get-tuple-element.20), channel_id=1, source_target_pairs={{4,0},{8,4},{12,8},{16,12},{20,16},{24,20},{28,24},{32,28},{36,32}... | collective-permute-start | bytes 53768 | tf_op jit(solution)/shard_map/ppermute | solution.py:25
  358.3 2.0 collective-permute-start.14
  358.6 4.3 %collective-permute-start.15 = (f32[5,34,1]{2,1,0:T(8,128)S(1)}, f32[5,34,1]{2,1,0:T(8,128)S(1)}, u32[]{:S(2)}, u32[]{:S(2)}) collective-permute-start(f32[5,34,1]{2,1,0:T(8,128)S(1)} %get-tuple-element.16), channel_id=1, source_target_pairs={{1,0},{2,1},{3,2},{0,3},{5,4},{6,5},{7,6},{4,7},{9,8},{10,9},{11,1... | collective-permute-start | bytes 2048 | tf_op jit(solution)/shard_map/ppermute | solution.py:25
  364.6 11.0 %collective-permute-start.16 = (f32[5,1,896]{2,1,0:T(1,128)S(1)}, f32[5,1,896]{2,1,0:T(1,128)S(1)}, u32[]{:S(2)}, u32[]{:S(2)}) collective-permute-start(f32[5,1,896]{2,1,0:T(1,128)S(1)} %get-tuple-element.19), channel_id=1, source_target_pairs={{0,4},{4,8},{8,12},{12,16},{16,20},{20,24},{24,28},{28,32},{32,36}... | collective-permute-start | bytes 53768 | tf_op jit(solution)/shard_map/ppermute | solution.py:24
  366.6 9.8 %collective-permute-start.17 = (f32[5,1,896]{2,1,0:T(1,128)S(1)}, f32[5,1,896]{2,1,0:T(1,128)S(1)}, u32[]{:S(2)}, u32[]{:S(2)}) collective-permute-start(f32[5,1,896]{2,1,0:T(1,128)S(1)} %get-tuple-element.18), channel_id=1, source_target_pairs={{4,0},{8,4},{12,8},{16,12},{20,16},{24,20},{28,24},{32,28},{36,32}... | collective-permute-start | bytes 53768 | tf_op jit(solution)/shard_map/ppermute | solution.py:25
  376.6 2.1 collective-permute-start.18
  377.0 4.1 %collective-permute-start.19 = (f32[5,34,1]{2,1,0:T(8,128)S(1)}, f32[5,34,1]{2,1,0:T(8,128)S(1)}, u32[]{:S(2)}, u32[]{:S(2)}) collective-permute-start(f32[5,34,1]{2,1,0:T(8,128)S(1)} %get-tuple-element.14), channel_id=1, source_target_pairs={{1,0},{2,1},{3,2},{0,3},{5,4},{6,5},{7,6},{4,7},{9,8},{10,9},{11,1... | collective-permute-start | bytes 2048 | tf_op jit(solution)/shard_map/ppermute | solution.py:25
  (11 other events, 151.0 us)
Sparse Core Ops, SparseCore 0:
  41.2 45.2 all-gather.2
  145.3 43.7 all-gather.4
where the time goes:
time: 394 us; the launch traced here: 390 us
  local copies, waits for them, and re-layouts  119 us (30%)
  waiting for transfers between devices  106 us (27%)
  starting transfers between devices  61 us (15%)
  matrix products  52.2 us (13%)
  other arithmetic  37 us (9%)
  between operations  14.9 us (4%)
    gather x2, local copies, waits for them, and re-layouts, per_device(): picked = jnp.take(bottom_rim.reshape(2, -1), flat_index, axis=1)  106 us
    all_gather x2, waiting for transfers between devices, per_device(): lax.all_gather(lines, 'lon', axis=1, tiled=True)  61.9 us
    ppermute x10, starting transfers between devices, padded_2(): after = lax.ppermute(first, axis, down)  43.2 us
    dot_general x2, matrix products, per_device(): jnp.dot(lax.all_gather(lines, 'lon', axis=1, tiled=True), basis, precisio...  41.9 us
    ppermute x10, waiting for transfers between devices, padded_2(): after = lax.ppermute(first, axis, down)  36.3 us
    ppermute x10, starting transfers between devices, padded_2(): before = lax.ppermute(last, axis, up)  17.6 us
    sin x1, other arithmetic, make_basis(): jnp.sin(2.0 * math.pi * sin_phase.astype(jnp.float32) / lon_total)  12.6 us
    cos x1, other arithmetic, make_basis(): jnp.cos(2.0 * math.pi * cos_phase.astype(jnp.float32) / lon_total)  11 us
  transfers between devices with their start and end apart: 22, of which 17 were waited for; matrix products, arithmetic and copies ran while one was open for 7% of the time, Pallas kernels for 0%

commit v1 on v0

--- a/solution.py
+++ b/solution.py
@@ -129,7 +129,9 @@
         )
         lines = tracer_now.reshape(line_count, lon_local)
         coeffs = jnp.dot(
-            lax.all_gather(lines, "lon", axis=1, tiled=True),
+            jnp.concatenate(
+                lax.all_to_all(jnp.stack([lines] * lax.axis_size("lon")), "lon", 0, 0), axis=1
+            ),
             basis,
             precision=highest,
             preferred_element_type=jnp.float32,

time: 394 us -> 411 us (1.043)
  local copies, waits for them, and re-layouts: 119 us -> 146 us
  starting transfers between devices: 61 us -> 76.1 us
  between operations: 14.9 us -> 1.56 us
  waiting for transfers between devices: 106 us -> 97.8 us
    all_gather x2 -> x0, waiting for transfers between devices: 61.9 us -> none  [per_device(): lax.all_gather(lines, 'lon', axis=1, tiled=True)]
    all_to_all x0 -> x2, waiting for transfers between devices: none -> 55.3 us  [per_device(): lax.all_to_all(jnp.stack([lines] * lax.axis_size('lon')), 'lon', 0, 0)]
    all_to_all x0 -> x2, starting transfers between devices: none -> 12.9 us  [per_device(): lax.all_to_all(jnp.stack([lines] * lax.axis_size('lon')), 'lon', 0, 0)]
    dot_general x0 -> x2, local copies, waits for them, and re-layouts: none -> 11.8 us  [per_device(): jnp.dot(jnp.concatenate(lax.all_to_all(jnp.stack([lines] * lax.axis_size(...]
    reshape x2, local copies, waits for them, and re-layouts: 3.8 us -> 12.5 us  [per_device(): jnp.concatenate(lax.all_to_all(jnp.stack([lines] * lax.axis_size('lon')),...]
    another operation x0 -> x4, local copies, waits for them, and re-layouts: none -> 8.11 us  [per_device(): jnp.stack([lines] * lax.axis_size('lon'))]
    ppermute x10, starting transfers between devices: 43.2 us -> 48.8 us  [padded_2(): after = lax.ppermute(first, axis, down)]
  transfers between devices with their start and end apart: 22 -> 22, of which waited for: 17 -> 16; matrix products, arithmetic and copies ran while one was open for 7% -> 7% of each run, Pallas kernels for 0% -> 0%
where the time goes in v1:
time: 411 us; the launch traced here: 406 us
  local copies, waits for them, and re-layouts  146 us (36%)
  waiting for transfers between devices  97.8 us (24%)
  starting transfers between devices  76.1 us (19%)
  matrix products  48.7 us (12%)
  other arithmetic  35.6 us (9%)
    gather x2, local copies, waits for them, and re-layouts, per_device(): picked = jnp.take(bottom_rim.reshape(2, -1), flat_index, axis=1)  106 us
    all_to_all x2, waiting for transfers between devices, per_device(): lax.all_to_all(jnp.stack([lines] * lax.axis_size('lon')), 'lon', 0, 0)  55.3 us
    ppermute x10, starting transfers between devices, padded_2(): after = lax.ppermute(first, axis, down)  48.8 us
    dot_general x2, matrix products, per_device(): jnp.dot(jnp.concatenate(lax.all_to_all(jnp.stack([lines] * lax.axis_size(...  38.4 us
    ppermute x10, waiting for transfers between devices, padded_2(): after = lax.ppermute(first, axis, down)  36.4 us
    ppermute x10, starting transfers between devices, padded_2(): before = lax.ppermute(last, axis, up)  14.3 us
    all_to_all x2, starting transfers between devices, per_device(): lax.all_to_all(jnp.stack([lines] * lax.axis_size('lon')), 'lon', 0, 0)  12.9 us
    reshape x2, local copies, waits for them, and re-layouts, per_device(): jnp.concatenate(lax.all_to_all(jnp.stack([lines] * lax.axis_size('lon')),...  12.5 us
  transfers between devices with their start and end apart: 22, of which 16 were waited for; matrix products, arithmetic and copies ran while one was open for 7% of the time, Pallas kernels for 0%

profile of v1, /device:TPU:3, one launch (start us, length us, event | category | flops | bytes accessed | tf_op | source)
XLA Modules:
  0.0 406.1 jit_solution(1494458569131659530)
XLA Ops:
  5.5 8.5 %collective-permute-start.1 = (f32[32,1,288]{2,1,0:T(1,128)S(1)}, f32[32,1,288]{2,1,0:T(1,128)S(1)}, u32[]{:S(2)}, u32[]{:S(2)}) collective-permute-start(f32[32,1,288]{2,1,0:T(1,128)S(1)} %get-tuple-element.13), channel_id=1, source_target_pairs={{4,0},{8,4},{12,8},{16,12},{20,16},{24,20},{28,24},{32,28},{36,32}... | collective-permute-start | bytes 110600 | tf_op jit(solution)/shard_map/ppermute | solution.py:25
  18.6 11.8 %collective-permute-done.2 = f32[32,26,1]{2,1,0:T(8,128)S(1)} collective-permute-done((f32[32,26,1]{2,1,0:T(8,128)S(1)}, f32[32,26,1]{2,1,0:T(8,128)S(1)}, u32[]{:S(2)}, u32[]{:S(2)}) %collective-permute-start.2) | collective-permute-done | bytes 3360 | tf_op jit(solution)/shard_map/ppermute | solution.py:25
  35.6 6.6 %all-to-all-start = ((f32[4,768,288]{1,2,0:T(8,128)}), f32[4,768,288]{1,2,0:T(8,128)}, u32[]{:S(2)}, u32[]{:S(2)}) async-start(f32[4,768,288]{1,2,0:T(8,128)} %stack.10), calls=%async_computation | async-start | bytes 7077888 | tf_op jit(solution)/shard_map/all_to_all | solution.py:133
  42.7 11.0 %fusion.5 = f32[1152,577]{1,0:T(8,128)S(1)} fusion(), kind=kLoop, calls=%fused_computation.11 | loop fusion | flops 5982336 | bytes 2658816 | tf_op jit(solution)/shard_map/cos | solution.py:51
  53.8 12.2 %fusion.8 = f32[1152,575]{1,0:T(8,128)} fusion(s32[575]{0:T(1024)S(1)} %iota_add_fusion), kind=kLoop, calls=%fused_computation.14 | loop fusion | flops 5961600 | bytes 2651900 | tf_op jit(solution)/shard_map/sin | solution.py:52
  66.0 16.4 %all-to-all-done = f32[4,768,288]{1,2,0:T(8,128)} async-done(((f32[4,768,288]{1,2,0:T(8,128)}), f32[4,768,288]{1,2,0:T(8,128)}, u32[]{:S(2)}, u32[]{:S(2)}) %all-to-all-start) | async-done | bytes 3538976 | tf_op jit(solution)/shard_map/all_to_all | solution.py:133
  82.4 6.3 %copy.33 = f32[768,4,288]{2,1,0:T(4,128)} copy(f32[768,4,288]{0,2,1:T(8,128)} %bitcast.1) | data formatting | bytes 7077888 | tf_op jit(solution)/shard_map/reshape | solution.py:132
  88.6 5.9 %dot_general.16 = f32[32,24,1152]{2,1,0:T(8,128)} reshape(f32[768,4,288]{2,1,0:T(4,128)} %copy.33) | data formatting | bytes 7077888 | tf_op jit(solution)/shard_map/dot_general | solution.py:131
  94.6 19.3 %convolution_multiply_fusion.1 = f32[32,24,1152]{2,1,0:T(8,128)S(1)} fusion(f32[32,24,1152]{2,1,0:T(8,128)} %dot_general.16, f32[1152,575]{1,0:T(8,128)} %fusion.8, f32[1152,577]{1,0:T(8,128)S(1)} %fusion.5, f32[24,1152]{1,0:T(8,128)S(1)} %fusion.90), kind=kOutput, calls=%fused_computation.8 | convolution fusion | flops 12232802304 | bytes 12496896 | tf_op jit(solution)/shard_map/dot_general | solution.py:131
  113.9 6.2 %fusion.16 = f32[32,24,288]{2,1,0:T(8,128)S(1)} fusion(f32[32,24,1152]{2,1,0:T(8,128)S(1)} %convolution_multiply_fusion.1, s32[]{:T(128)S(6)} %select_n.72, f32[1152,577]{1,0:T(8,128)S(1)} %fusion.5, f32[1152,575]{1,0:T(8,128)S(1)} %copy-done), kind=kOutput, calls=%fused_computation.24 | convolution fusion | flops 3057979392 | bytes 9732100 | tf_op jit(solution)/shard_map/dot_general | solution.py:81
  122.3 9.1 %collective-permute-start.5 = (f32[32,1,288]{2,1,0:T(1,128)S(1)}, f32[32,1,288]{2,1,0:T(1,128)S(1)}, u32[]{:S(2)}, u32[]{:S(2)}) collective-permute-start(f32[32,1,288]{2,1,0:T(1,128)S(1)} %get-tuple-element.11), channel_id=1, source_target_pairs={{4,0},{8,4},{12,8},{16,12},{20,16},{24,20},{28,24},{32,28},{36,32}... | collective-permute-start | bytes 110600 | tf_op jit(solution)/shard_map/ppermute | solution.py:25
  134.8 11.4 %collective-permute-done.6 = f32[32,26,1]{2,1,0:T(8,128)S(1)} collective-permute-done((f32[32,26,1]{2,1,0:T(8,128)S(1)}, f32[32,26,1]{2,1,0:T(8,128)S(1)}, u32[]{:S(2)}, u32[]{:S(2)}) %collective-permute-start.6) | collective-permute-done | bytes 3360 | tf_op jit(solution)/shard_map/ppermute | solution.py:25
  154.6 6.3 %all-to-all-start.1 = ((f32[4,768,288]{1,2,0:T(8,128)}), f32[4,768,288]{1,2,0:T(8,128)}, u32[]{:S(2)}, u32[]{:S(2)}) async-start(f32[4,768,288]{1,2,0:T(8,128)} %stack.11), calls=%async_computation.1 | async-start | bytes 7077888 | tf_op jit(solution)/shard_map/all_to_all | solution.py:133
  162.2 38.9 %all-to-all-done.1 = f32[4,768,288]{1,2,0:T(8,128)} async-done(((f32[4,768,288]{1,2,0:T(8,128)}), f32[4,768,288]{1,2,0:T(8,128)}, u32[]{:S(2)}, u32[]{:S(2)}) %all-to-all-start.1) | async-done | bytes 3538976 | tf_op jit(solution)/shard_map/all_to_all | solution.py:133
  201.2 6.3 %copy.35 = f32[768,4,288]{2,1,0:T(4,128)} copy(f32[768,4,288]{0,2,1:T(8,128)} %bitcast.5) | data formatting | bytes 7077888 | tf_op jit(solution)/shard_map/reshape | solution.py:132
  207.4 5.9 %dot_general.19 = f32[32,24,1152]{2,1,0:T(8,128)} reshape(f32[768,4,288]{2,1,0:T(4,128)} %copy.35) | data formatting | bytes 7077888 | tf_op jit(solution)/shard_map/dot_general | solution.py:131
  213.4 19.1 %convolution_multiply_fusion = f32[32,24,1152]{2,1,0:T(8,128)S(1)} fusion(f32[32,24,1152]{2,1,0:T(8,128)} %dot_general.19, f32[1152,575]{1,0:T(8,128)} %fusion.8, f32[1152,577]{1,0:T(8,128)S(1)} %fusion.5, f32[24,1152]{1,0:T(8,128)S(1)} %copy-done.12), kind=kOutput, calls=%fused_computation.7 | convolution fusion | flops 12232802304 | bytes 12496896 | tf_op jit(solution)/shard_map/dot_general | solution.py:131
  232.5 4.1 %fusion.93 = f32[768,288]{0,1:T(8,128)S(1)} fusion(f32[768,1152]{1,0:T(8,128)S(1)} %bitcast.62, s32[]{:T(128)S(6)} %select_n.72, f32[1152,577]{1,0:T(8,128)S(1)} %fusion.5, f32[1152,575]{1,0:T(8,128)S(1)} %copy-done.1), kind=kOutput, calls=%fused_computation.185 | convolution fusion | flops 3057979392 | bytes 9732100 | tf_op jit(solution)/shard_map/dot_general | solution.py:81
  239.9 8.6 %collective-permute-start.9 = (f32[2,1,288]{1,2,0:T(8,128)S(1)}, f32[2,1,288]{1,2,0:T(8,128)S(1)}, u32[]{:S(2)}, u32[]{:S(2)}) collective-permute-start(f32[2,1,288]{1,2,0:T(8,128)S(1)} %get-tuple-element.31), channel_id=1, source_target_pairs={{4,0},{8,4},{12,8},{16,12},{20,16},{24,20},{28,24},{32,28},{36,32}... | collective-permute-start | bytes 6920 | tf_op jit(solution)/shard_map/ppermute | solution.py:25
  248.6 4.3 %collective-permute-done.8 = f32[2,1,288]{1,2,0:T(8,128)S(1)} collective-permute-done((f32[2,1,288]{1,2,0:T(8,128)S(1)}, f32[2,1,288]{1,2,0:T(8,128)S(1)}, u32[]{:S(2)}, u32[]{:S(2)}) %collective-permute-start.8) | collective-permute-done | bytes 2336 | tf_op jit(solution)/shard_map/ppermute | solution.py:24
  262.0 96.8 %gather_fusion = f32[28672,2]{1,0:T(8,128)} fusion(f32[2,7540]{0,1:T(8,128)} %copy.43, s32[28672]{0:T(1024)S(1)} %broadcast_clamp_fusion), kind=kCustom, calls=%fused_computation | custom fusion | bytes 573440 | tf_op jit(solution)/shard_map/jit(_take)/gather | solution.py:150
  358.8 9.0 %copy.44 = f32[32,896,2]{1,0,2:T(8,128)S(1)} copy(f32[32,896,2]{2,1,0:T(8,128)} %bitcast.59) | data formatting | bytes 458752 | tf_op jit(solution)/shard_map/jit(_take)/gather | solution.py:150
  369.9 9.2 %collective-permute-start.13 = (f32[5,1,896]{2,1,0:T(1,128)S(1)}, f32[5,1,896]{2,1,0:T(1,128)S(1)}, u32[]{:S(2)}, u32[]{:S(2)}) collective-permute-start(f32[5,1,896]{2,1,0:T(1,128)S(1)} %get-tuple-element.20), channel_id=1, source_target_pairs={{4,0},{8,4},{12,8},{16,12},{20,16},{24,20},{28,24},{32,28},{36,32}... | collective-permute-start | bytes 53768 | tf_op jit(solution)/shard_map/ppermute | solution.py:25
  388.9 8.6 %collective-permute-start.17 = (f32[5,1,896]{2,1,0:T(1,128)S(1)}, f32[5,1,896]{2,1,0:T(1,128)S(1)}, u32[]{:S(2)}, u32[]{:S(2)}) collective-permute-start(f32[5,1,896]{2,1,0:T(1,128)S(1)} %get-tuple-element.18), channel_id=1, source_target_pairs={{4,0},{8,4},{12,8},{16,12},{20,16},{24,20},{28,24},{32,28},{36,32}... | collective-permute-start | bytes 53768 | tf_op jit(solution)/shard_map/ppermute | solution.py:25
  (126 shorter events, 62.7 us)
Async XLA Ops:
  0.6 29.8 %copy-start.2 = (f32[32,24,288]{2,1,0:T(8,128)S(1)}, f32[32,24,288]{2,1,0:T(8,128)}, u32[]{:S(2)}) copy-start(f32[32,24,288]{2,1,0:T(8,128)} %param.8) | copy-start | bytes 2654212
  2.0 12.0 %collective-permute-start = (f32[32,1,288]{2,1,0:T(1,128)S(1)}, f32[32,1,288]{2,1,0:T(1,128)S(1)}, u32[]{:S(2)}, u32[]{:S(2)}) collective-permute-start(f32[32,1,288]{2,1,0:T(1,128)S(1)} %get-tuple-element.12), channel_id=1, source_target_pairs={{0,4},{4,8},{8,12},{12,16},{16,20},{20,24},{24,28},{28,32},{32,36}... | collective-permute-start | bytes 110600 | tf_op jit(solution)/shard_map/ppermute | solution.py:24
  5.5 9.6 %collective-permute-start.1 = (f32[32,1,288]{2,1,0:T(1,128)S(1)}, f32[32,1,288]{2,1,0:T(1,128)S(1)}, u32[]{:S(2)}, u32[]{:S(2)}) collective-permute-start(f32[32,1,288]{2,1,0:T(1,128)S(1)} %get-tuple-element.13), channel_id=1, source_target_pairs={{4,0},{8,4},{12,8},{16,12},{20,16},{24,20},{28,24},{32,28},{36,32}... | collective-permute-start | bytes 110600 | tf_op jit(solution)/shard_map/ppermute | solution.py:25
  16.6 13.8 %collective-permute-start.2 = (f32[32,26,1]{2,1,0:T(8,128)S(1)}, f32[32,26,1]{2,1,0:T(8,128)S(1)}, u32[]{:S(2)}, u32[]{:S(2)}) collective-permute-start(f32[32,26,1]{2,1,0:T(8,128)S(1)} %get-tuple-element.9), channel_id=1, source_target_pairs={{1,0},{2,1},{3,2},{0,3},{5,4},{6,5},{7,6},{4,7},{9,8},{10,9},{11,1... | collective-permute-start | bytes 9992 | tf_op jit(solution)/shard_map/ppermute | solution.py:25
  18.2 12.2 %collective-permute-start.3 = (f32[32,26,1]{2,1,0:T(8,128)S(1)}, f32[32,26,1]{2,1,0:T(8,128)S(1)}, u32[]{:S(2)}, u32[]{:S(2)}) collective-permute-start(f32[32,26,1]{2,1,0:T(8,128)S(1)} %get-tuple-element.8), channel_id=1, source_target_pairs={{0,1},{1,2},{2,3},{3,0},{4,5},{5,6},{6,7},{7,4},{8,9},{9,10},{10,1... | collective-permute-start | bytes 9992 | tf_op jit(solution)/shard_map/ppermute | solution.py:24
  35.6 46.8 %all-to-all-start = ((f32[4,768,288]{1,2,0:T(8,128)}), f32[4,768,288]{1,2,0:T(8,128)}, u32[]{:S(2)}, u32[]{:S(2)}) async-start(f32[4,768,288]{1,2,0:T(8,128)} %stack.10), calls=%async_computation | async-start | bytes 7077888 | tf_op jit(solution)/shard_map/all_to_all | solution.py:133
  53.8 40.8 %copy-start.11 = (f32[24,1152]{1,0:T(8,128)}, f32[24,1152]{1,0:T(8,128)S(1)}, u32[]{:S(2)}) copy-start(f32[24,1152]{1,0:T(8,128)S(1)} %fusion.90) | copy-start | bytes 331780
  120.2 11.2 %collective-permute-start.4 = (f32[32,1,288]{2,1,0:T(1,128)S(1)}, f32[32,1,288]{2,1,0:T(1,128)S(1)}, u32[]{:S(2)}, u32[]{:S(2)}) collective-permute-start(f32[32,1,288]{2,1,0:T(1,128)S(1)} %get-tuple-element.10), channel_id=1, source_target_pairs={{0,4},{4,8},{8,12},{12,16},{16,20},{20,24},{24,28},{28,32},{32,36}... | collective-permute-start | bytes 110600 | tf_op jit(solution)/shard_map/ppermute | solution.py:24
  122.3 10.2 %collective-permute-start.5 = (f32[32,1,288]{2,1,0:T(1,128)S(1)}, f32[32,1,288]{2,1,0:T(1,128)S(1)}, u32[]{:S(2)}, u32[]{:S(2)}) collective-permute-start(f32[32,1,288]{2,1,0:T(1,128)S(1)} %get-tuple-element.11), channel_id=1, source_target_pairs={{4,0},{8,4},{12,8},{16,12},{20,16},{24,20},{28,24},{32,28},{36,32}... | collective-permute-start | bytes 110600 | tf_op jit(solution)/shard_map/ppermute | solution.py:25
  132.8 13.4 %collective-permute-start.6 = (f32[32,26,1]{2,1,0:T(8,128)S(1)}, f32[32,26,1]{2,1,0:T(8,128)S(1)}, u32[]{:S(2)}, u32[]{:S(2)}) collective-permute-start(f32[32,26,1]{2,1,0:T(8,128)S(1)} %get-tuple-element.7), channel_id=1, source_target_pairs={{1,0},{2,1},{3,2},{0,3},{5,4},{6,5},{7,6},{4,7},{9,8},{10,9},{11,1... | collective-permute-start | bytes 9992 | tf_op jit(solution)/shard_map/ppermute | solution.py:25
  134.8 11.6 %collective-permute-start.7 = (f32[32,26,1]{2,1,0:T(8,128)S(1)}, f32[32,26,1]{2,1,0:T(8,128)S(1)}, u32[]{:S(2)}, u32[]{:S(2)}) collective-permute-start(f32[32,26,1]{2,1,0:T(8,128)S(1)} %get-tuple-element.6), channel_id=1, source_target_pairs={{0,1},{1,2},{2,3},{3,0},{4,5},{5,6},{6,7},{7,4},{8,9},{9,10},{10,1... | collective-permute-start | bytes 9992 | tf_op jit(solution)/shard_map/ppermute | solution.py:24
  154.6 46.6 %all-to-all-start.1 = ((f32[4,768,288]{1,2,0:T(8,128)}), f32[4,768,288]{1,2,0:T(8,128)}, u32[]{:S(2)}, u32[]{:S(2)}) async-start(f32[4,768,288]{1,2,0:T(8,128)} %stack.11), calls=%async_computation.1 | async-start | bytes 7077888 | tf_op jit(solution)/shard_map/all_to_all | solution.py:133
  237.8 15.1 %collective-permute-start.8 = (f32[2,1,288]{1,2,0:T(8,128)S(1)}, f32[2,1,288]{1,2,0:T(8,128)S(1)}, u32[]{:S(2)}, u32[]{:S(2)}) collective-permute-start(f32[2,1,288]{1,2,0:T(8,128)S(1)} %get-tuple-element.30), channel_id=1, source_target_pairs={{0,4},{4,8},{8,12},{12,16},{16,20},{20,24},{24,28},{28,32},{32,36}... | collective-permute-start | bytes 6920 | tf_op jit(solution)/shard_map/ppermute | solution.py:24
  239.9 13.9 %collective-permute-start.9 = (f32[2,1,288]{1,2,0:T(8,128)S(1)}, f32[2,1,288]{1,2,0:T(8,128)S(1)}, u32[]{:S(2)}, u32[]{:S(2)}) collective-permute-start(f32[2,1,288]{1,2,0:T(8,128)S(1)} %get-tuple-element.31), channel_id=1, source_target_pairs={{4,0},{8,4},{12,8},{16,12},{20,16},{24,20},{28,24},{32,28},{36,32}... | collective-permute-start | bytes 6920 | tf_op jit(solution)/shard_map/ppermute | solution.py:25
  254.1 2.6 collective-permute-start.10
  255.7 3.3 collective-permute-start.11
  368.0 11.2 %collective-permute-start.12 = (f32[5,1,896]{2,1,0:T(1,128)S(1)}, f32[5,1,896]{2,1,0:T(1,128)S(1)}, u32[]{:S(2)}, u32[]{:S(2)}) collective-permute-start(f32[5,1,896]{2,1,0:T(1,128)S(1)} %get-tuple-element.21), channel_id=1, source_target_pairs={{0,4},{4,8},{8,12},{12,16},{16,20},{20,24},{24,28},{28,32},{32,36}... | collective-permute-start | bytes 53768 | tf_op jit(solution)/shard_map/ppermute | solution.py:24
  369.9 10.1 %collective-permute-start.13 = (f32[5,1,896]{2,1,0:T(1,128)S(1)}, f32[5,1,896]{2,1,0:T(1,128)S(1)}, u32[]{:S(2)}, u32[]{:S(2)}) collective-permute-start(f32[5,1,896]{2,1,0:T(1,128)S(1)} %get-tuple-element.20), channel_id=1, source_target_pairs={{4,0},{8,4},{12,8},{16,12},{20,16},{24,20},{28,24},{32,28},{36,32}... | collective-permute-start | bytes 53768 | tf_op jit(solution)/shard_map/ppermute | solution.py:25
  380.2 2.0 collective-permute-start.14
  380.5 4.7 %collective-permute-start.15 = (f32[5,34,1]{2,1,0:T(8,128)S(1)}, f32[5,34,1]{2,1,0:T(8,128)S(1)}, u32[]{:S(2)}, u32[]{:S(2)}) collective-permute-start(f32[5,34,1]{2,1,0:T(8,128)S(1)} %get-tuple-element.16), channel_id=1, source_target_pairs={{1,0},{2,1},{3,2},{0,3},{5,4},{6,5},{7,6},{4,7},{9,8},{10,9},{11,1... | collective-permute-start | bytes 2048 | tf_op jit(solution)/shard_map/ppermute | solution.py:25
  386.9 10.7 %collective-permute-start.16 = (f32[5,1,896]{2,1,0:T(1,128)S(1)}, f32[5,1,896]{2,1,0:T(1,128)S(1)}, u32[]{:S(2)}, u32[]{:S(2)}) collective-permute-start(f32[5,1,896]{2,1,0:T(1,128)S(1)} %get-tuple-element.19), channel_id=1, source_target_pairs={{0,4},{4,8},{8,12},{12,16},{16,20},{20,24},{24,28},{28,32},{32,36}... | collective-permute-start | bytes 53768 | tf_op jit(solution)/shard_map/ppermute | solution.py:24
  388.9 9.5 %collective-permute-start.17 = (f32[5,1,896]{2,1,0:T(1,128)S(1)}, f32[5,1,896]{2,1,0:T(1,128)S(1)}, u32[]{:S(2)}, u32[]{:S(2)}) collective-permute-start(f32[5,1,896]{2,1,0:T(1,128)S(1)} %get-tuple-element.18), channel_id=1, source_target_pairs={{4,0},{8,4},{12,8},{16,12},{20,16},{24,20},{28,24},{32,28},{36,32}... | collective-permute-start | bytes 53768 | tf_op jit(solution)/shard_map/ppermute | solution.py:25
  398.6 2.1 collective-permute-start.18
  398.9 4.8 %collective-permute-start.19 = (f32[5,34,1]{2,1,0:T(8,128)S(1)}, f32[5,34,1]{2,1,0:T(8,128)S(1)}, u32[]{:S(2)}, u32[]{:S(2)}) collective-permute-start(f32[5,34,1]{2,1,0:T(8,128)S(1)} %get-tuple-element.14), channel_id=1, source_target_pairs={{1,0},{2,1},{3,2},{0,3},{5,4},{6,5},{7,6},{4,7},{9,8},{10,9},{11,1... | collective-permute-start | bytes 2048 | tf_op jit(solution)/shard_map/ppermute | solution.py:25
  (14 other events, 203.1 us)
